TPU v7x, 512 devices: a whole 4x8x8 slice. The times are simulated.
512 devices in a mesh: tm: 64 (over y_lo, z, core), user: 8 (over x, y_hi).
Axes of the slice: x: 4, y: 8 (y_hi: 2, y_lo: 4; y = y_hi * 4 + y_lo), z: 8, core: 2. Of those that a mesh axis runs over, the one named last changes fastest.
Arguments:
- events: bfloat16 [256, 4096, 256], P('user', 'tm'), parts along dimension 0, may hold values from -6 to 6
- lengths: int32 [256], P('user'), parts along dimension 0, may hold values from 1024 to 4096
- w_mix: bfloat16 [2, 256, 256], replicated, may hold values from -0.375 to 0.375
- w_context: bfloat16 [2, 256, 256], replicated, may hold values from -0.375 to 0.375
- gains: float32 [2, 256], replicated, may hold values from 0.5 to 1.5
- w_up: bfloat16 [2, 256, 1024], replicated, may hold values from -0.375 to 0.375
- w_down: bfloat16 [2, 1024, 256], replicated, may hold values from -0.1875 to 0.1875
Outputs:
- encoded: bfloat16 [256, 4096, 256], P('user', 'tm'), parts along dimension 0
There are 8 independent parts, one for each index of `user`. A program takes and returns all parts, laid end to end along the dimension named above; an argument that names none is the same for every part. Nothing has to cross between parts.
All inputs are finite; a program needn't handle non-finite values.
Results may differ from a plain program's by a relative error of at most 0.012.
Values may be sent and summed in bfloat16 or wider, within the bound.
No kernel may reach another device: no remote copies, remote signals or barrier semaphores. Data moves between devices by JAX's collectives and lax.ppermute only.
A program may use at most 64 MiB of HBM per device.

v0:
```python
import jax
import jax.numpy as jnp
from jax import lax
from jax.sharding import Mesh
from jax.sharding import PartitionSpec as P

D = 256
HALF = 32
LAYERS = 2
TM = ("tm_0", "tm_1", "tm_2")


def neutral_like(shard, identity):
    return jnp.broadcast_to(jnp.asarray(identity, shard.dtype), shard.shape)


def carried_in(shard, axes, combine, identity):
    before = start = neutral_like(shard, identity)
    total = shard
    for axis in reversed(axes):
        devices, index = (lax.axis_size(axis), lax.axis_index(axis))
        pieces = lax.all_gather(total, axis)
        inside, total = (start, start)
        for k in range(devices):
            passed = k < index
            total = combine(total, pieces[k])
            inside = jnp.where(passed, total, inside)
        before = combine(inside, before)
    return before


def with_halo(block, sides, width):
    for axis, dim in sides:
        count = lax.axis_size(axis)
        forward = [(i, i + 1) for i in range(count - 1)]
        backward = [(target, source) for source, target in forward]
        low = lax.ppermute(
            lax.slice_in_dim(block, block.shape[dim] - width, None, axis=dim), axis, forward
        )
        high = lax.ppermute(lax.slice_in_dim(block, 0, width, axis=dim), axis, backward)
        block = jnp.concatenate([low, block, high], axis=dim)
    return block


def add_pair(earlier, later):
    return earlier + later


def earlier_sums(totals):
    return carried_in(totals, TM, add_pair, jnp.zeros_like(totals))


def per_device(events, lengths, w_mix, w_context, gains, w_up, w_down):
    own_rows = events.shape[1]
    first_pos = lax.axis_index(TM) * own_rows

    def valid_at(row_count):
        position = first_pos + jnp.arange(row_count, dtype=jnp.int32)
        return (position[None, :] >= 0) & (position[None, :] < lengths[:, None])

    current = jnp.where(valid_at(own_rows)[..., None], events, jnp.zeros_like(events))
    for layer_index in range(LAYERS):
        extended = with_halo(current, ((TM, 1),), HALF)
        own_part = current
        totals = jnp.sum(own_part, axis=1, dtype=jnp.float32)
        earlier = earlier_sums(totals)
        before = jnp.sum(current[:, :0], axis=1, dtype=jnp.float32)
        context_row_count = current.shape[1]
        index_rows = jnp.arange(context_row_count, dtype=jnp.int32)
        lower_ones = (index_rows[:, None] >= index_rows[None, :]).astype(jnp.bfloat16)
        running = jnp.einsum("ts,usd->utd", lower_ones, current, preferred_element_type=jnp.float32)
        running = running + (earlier - before)[:, None, :]
        context_position = (first_pos - 0 + index_rows).astype(jnp.float32)
        scale = 1.0 / jnp.sqrt(jnp.maximum(context_position + 1.0, 1.0))
        context = (running * scale[None, :, None]).astype(jnp.bfloat16)
        apply_row_count = extended.shape[1] - 2 * HALF
        center = extended[:, HALF : HALF + apply_row_count]
        scores = (
            jnp.einsum("utd,usd->uts", center, extended, preferred_element_type=jnp.float32) / D
        )
        target = jnp.arange(apply_row_count, dtype=jnp.int32)[:, None]
        source = jnp.arange(extended.shape[1], dtype=jnp.int32)[None, :]
        in_band = (source >= target) & (source <= target + 2 * HALF)
        weights = jnp.where(in_band[None], scores, 0.0).astype(jnp.bfloat16)
        mixed_rows = jnp.einsum(
            "uts,usd->utd", weights, extended, preferred_element_type=jnp.float32
        ).astype(jnp.bfloat16)
        compressed = jnp.dot(mixed_rows, w_mix[layer_index], preferred_element_type=jnp.float32)
        compressed = compressed + jnp.dot(
            context, w_context[layer_index], preferred_element_type=jnp.float32
        )
        summed = center.astype(jnp.float32) + compressed
        row_mean = jnp.mean(summed, axis=-1, keepdims=True)
        row_var = jnp.mean((summed - row_mean) ** 2, axis=-1, keepdims=True)
        normed = ((summed - row_mean) / jnp.sqrt(row_var + 1e-05) * gains[layer_index]).astype(
            jnp.bfloat16
        )
        hidden = jax.nn.relu(
            jnp.dot(normed, w_up[layer_index], preferred_element_type=jnp.float32)
        ).astype(jnp.bfloat16)
        result = normed.astype(jnp.float32) + jnp.dot(
            hidden, w_down[layer_index], preferred_element_type=jnp.float32
        )
        valid_mask = valid_at(apply_row_count)
        current = jnp.where(valid_mask[..., None], result, 0.0).astype(jnp.bfloat16)
    return current


def solution(mesh):
    torus = Mesh(
        mesh.devices.reshape(4, 8, 2, mesh.shape["user"]), ("tm_0", "tm_1", "tm_2", "user")
    )
    return jax.shard_map(
        per_device,
        mesh=torus,
        in_specs=(P("user", TM, None), P("user"), P(), P(), P(), P(), P()),
        out_specs=P("user", TM, None),
        check_vma=False,
    )
```

profile of v0, /device:TPU:56, one launch (start us, length us, event | category | flops | bytes accessed | tf_op | source)
XLA Modules:
  0.0 133.2 jit_solution(14766187348028739984)
XLA Ops:
  0.0 0.7 compare_and_fusion
  0.7 1.6 %convert_reduce_fusion.1 = (f32[32,256]{1,0:T(8,128)S(1)}, bf16[32,64,256]{2,1,0:T(8,128)(2,1)S(1)}) fusion(bf16[32,64,256]{2,1,0:T(8,128)(2,1)} %param.7, pred[32,64]{1,0:T(8,128)(4,1)S(1)} %compare_and_fusion), kind=kLoop, calls=%fused_computation.11 | loop fusion | flops 1564672 | bytes 2131968 | tf_op jit(solution)/shard_map/reduce_sum | solution.py:65
  2.3 0.1 fusion.87
  2.4 11.2 %collective-permute-start.1 = (bf16[32,32,256]{2,1,0:T(8,128)(2,1)S(1)}, bf16[32,32,256]{2,1,0:T(8,128)(2,1)S(1)}, u32[]{:S(2)}, u32[]{:S(2)}) collective-permute-start(bf16[32,32,256]{2,1,0:T(8,128)(2,1)S(1)} %get-tuple-element.14), channel_id=1, source_target_pairs={{8,0},{16,8},{24,16},{32,24},{40,32},{48,40},{56,48},{64,56},{72,6... | collective-permute-start | bytes 1572872 | tf_op jit(solution)/shard_map/ppermute | solution.py:40
  13.6 1.9 %collective-permute-start = (bf16[32,32,256]{2,1,0:T(8,128)(2,1)S(1)}, bf16[32,32,256]{2,1,0:T(8,128)(2,1)}, u32[]{:S(2)}, u32[]{:S(2)}) collective-permute-start(bf16[32,32,256]{2,1,0:T(8,128)(2,1)S(1)} %get-tuple-element.13), channel_id=1, source_target_pairs={{0,8},{8,16},{16,24},{24,32},{32,40},{40,48},{48,56},{56,64},{64,7... | collective-permute-start | bytes 1572872 | tf_op jit(solution)/shard_map/ppermute | solution.py:37
  15.5 1.9 %all-gather = f32[64,256]{1,0:T(8,128)S(1)} all-gather(f32[32,256]{1,0:T(8,128)S(1)} %get-tuple-element.9), channel_id=2, replica_groups=mesh['tm_0'=4,'tm_1'=8,'tm_2'=2,'user'=8] {'tm_2'}, dimensions={0}, use_global_device_ids=true | all-gather | bytes 98304 | tf_op jit(solution)/shard_map/all_gather | solution.py:22
  17.4 28.5 %all-gather.2 = f32[256,256]{1,0:T(8,128)S(1)} all-gather(f32[32,256]{1,0:T(8,128)S(1)} %slice_add_fusion.17), channel_id=4, replica_groups=mesh['tm_0'=4,'tm_1'=8,'tm_2'=2,'user'=8] {'tm_1'}, dimensions={0}, use_global_device_ids=true | all-gather | bytes 294912 | tf_op jit(solution)/shard_map/all_gather | solution.py:22
  45.9 13.4 %all_gather.31 = f32[4,32,256]{2,1,0:T(8,128)S(1)} all-gather(f32[1,32,256]{2,1,0:T(8,128)S(1)} %get-tuple-element.7), channel_id=1, replica_groups=mesh['tm_0'=4,'tm_1'=8,'tm_2'=2,'user'=8] {'tm_0'}, dimensions={0}, use_global_device_ids=true | all-gather | bytes 163840 | tf_op jit(solution)/shard_map/all_gather | solution.py:22
  59.5 1.9 %fusion.19 = bf16[32,64,128]{2,1,0:T(8,128)(2,1)S(1)} fusion(bf16[32,64,256]{2,1,0:T(8,128)(2,1)S(1)} %get-tuple-element.10, bf16[32,32,256]{2,1,0:T(8,128)(2,1)S(1)} %collective-permute-done.1, bf16[32,32,256]{2,1,0:T(8,128)(2,1)} %collective-permute-done, pred[64,128]{1,0:T(8,128)(4,1)S(1)} %fusion.72), kind=kOutput, calls=%fused_computation.35 | convolution fusion | flops 141295616 | bytes 2629632 | tf_op jit(solution)/shard_map/utd,usd->uts/dot_general | solution.py:79
  61.5 3.2 %fusion.12 = f32[32,64,256]{2,1,0:T(8,128)} fusion(bf16[32,64,128]{2,1,0:T(8,128)(2,1)S(1)} %fusion.19, bf16[32,32,256]{2,1,0:T(8,128)(2,1)S(1)} %collective-permute-done.1, bf16[32,64,256]{2,1,0:T(8,128)(2,1)S(1)} %get-tuple-element.10, bf16[32,32,256]{2,1,0:T(8,128)(2,1)} %collective-permute-done, bf16[2,256,256]{2,1,0:T(8,128)(2,1)S(1)} %copy-done.4), kind=kOutput, calls=%fused_computation.28 | convolution fusion | flops 409468928 | bytes 4849664 | tf_op jit(solution)/shard_map/dot_general | solution.py:88
  64.7 2.4 %fusion.89 = (f32[32,64]{1,0:T(8,128)S(1)}, f32[32,64,256]{2,1,0:T(8,128)S(1)}) fusion(f32[32,64,256]{2,1,0:T(8,128)} %fusion.12, bf16[2,256,256]{2,1,0:T(8,128)(2,1)S(1)} %copy-done.1, bf16[32,64,256]{2,1,0:T(8,128)(2,1)S(1)} %get-tuple-element.10, f32[64]{0:T(128)S(1)} %maximum_rsqrt_fusion, f32[32,256]{1,0:T(8,128)S(1)} %fusion.64), kind=kOutput, calls=%fused_computation.128 | convolution fusion | flops 339216384 | bytes 6464000 | tf_op jit(solution)/shard_map/dot_general | solution.py:89
  67.1 0.6 multiply_reduce_fusion.1
  67.8 3.9 %convert_reduce_fusion = (f32[32,256]{1,0:T(8,128)S(1)}, bf16[32,64,256]{2,1,0:T(8,128)(2,1)S(1)}) fusion(bf16[2,1024,256]{2,1,0:T(8,128)(2,1)} %param.13, f32[32,64,256]{2,1,0:T(8,128)S(1)} %get-tuple-element.18, f32[256]{0:T(256)S(1)} %bitcast.145, f32[32,64]{1,0:T(8,128)S(1)} %add_sqrt_fusion.1, f32[32,64]{1,0:T(8,128)S(1)} %broadcast_multiply_fusion.1, ...), kind=kOutput, calls=%fused_computation.9 | convolution fusion | flops 2159009792 | bytes 6395904 | tf_op jit(solution)/shard_map/dot_general | solution.py:101
  71.8 1.9 %collective-permute-start.3 = (bf16[32,32,256]{2,1,0:T(8,128)(2,1)S(1)}, bf16[32,32,256]{2,1,0:T(8,128)(2,1)S(1)}, u32[]{:S(2)}, u32[]{:S(2)}) collective-permute-start(bf16[32,32,256]{2,1,0:T(8,128)(2,1)S(1)} %get-tuple-element.12), channel_id=1, source_target_pairs={{8,0},{16,8},{24,16},{32,24},{40,32},{48,40},{56,48},{64,56},{72,6... | collective-permute-start | bytes 1572872 | tf_op jit(solution)/shard_map/ppermute | solution.py:40
  73.7 2.4 %collective-permute-start.2 = (bf16[32,32,256]{2,1,0:T(8,128)(2,1)S(1)}, bf16[32,32,256]{2,1,0:T(8,128)(2,1)S(1)}, u32[]{:S(2)}, u32[]{:S(2)}) collective-permute-start(bf16[32,32,256]{2,1,0:T(8,128)(2,1)S(1)} %get-tuple-element.11), channel_id=1, source_target_pairs={{0,8},{8,16},{16,24},{24,32},{32,40},{40,48},{48,56},{56,64},{64,7... | collective-permute-start | bytes 1572872 | tf_op jit(solution)/shard_map/ppermute | solution.py:37
  76.1 1.9 %all-gather.1 = f32[64,256]{1,0:T(8,128)S(1)} all-gather(f32[32,256]{1,0:T(8,128)S(1)} %get-tuple-element.19), channel_id=3, replica_groups=mesh['tm_0'=4,'tm_1'=8,'tm_2'=2,'user'=8] {'tm_2'}, dimensions={0}, use_global_device_ids=true | all-gather | bytes 98304 | tf_op jit(solution)/shard_map/all_gather | solution.py:22
  78.0 28.0 %all-gather.3 = f32[256,256]{1,0:T(8,128)S(1)} all-gather(f32[32,256]{1,0:T(8,128)S(1)} %slice_add_fusion.8), channel_id=5, replica_groups=mesh['tm_0'=4,'tm_1'=8,'tm_2'=2,'user'=8] {'tm_1'}, dimensions={0}, use_global_device_ids=true | all-gather | bytes 294912 | tf_op jit(solution)/shard_map/all_gather | solution.py:22
  106.0 13.6 %all_gather.35 = f32[4,32,256]{2,1,0:T(8,128)S(1)} all-gather(f32[1,32,256]{2,1,0:T(8,128)S(1)} %get-tuple-element.5), channel_id=1, replica_groups=mesh['tm_0'=4,'tm_1'=8,'tm_2'=2,'user'=8] {'tm_0'}, dimensions={0}, use_global_device_ids=true | all-gather | bytes 163840 | tf_op jit(solution)/shard_map/all_gather | solution.py:22
  119.6 1.6 %fusion.17 = bf16[32,64,128]{2,1,0:T(8,128)(2,1)} fusion(bf16[32,64,256]{2,1,0:T(8,128)(2,1)S(1)} %get-tuple-element.20, bf16[32,32,256]{2,1,0:T(8,128)(2,1)S(1)} %collective-permute-done.3, bf16[32,32,256]{2,1,0:T(8,128)(2,1)S(1)} %collective-permute-done.2, pred[64,128]{1,0:T(8,128)(4,1)S(1)} %fusion.72), kind=kOutput, calls=%fused_computation.33 | convolution fusion | flops 141295616 | bytes 2629632 | tf_op jit(solution)/shard_map/utd,usd->uts/dot_general | solution.py:79
  121.2 3.1 %fusion.13 = f32[32,64,256]{2,1,0:T(8,128)} fusion(bf16[32,64,128]{2,1,0:T(8,128)(2,1)} %fusion.17, bf16[32,32,256]{2,1,0:T(8,128)(2,1)S(1)} %collective-permute-done.3, bf16[32,64,256]{2,1,0:T(8,128)(2,1)S(1)} %get-tuple-element.20, bf16[32,32,256]{2,1,0:T(8,128)(2,1)S(1)} %collective-permute-done.2, bf16[2,256,256]{2,1,0:T(8,128)(2,1)S(1)} %copy-done.5), kind=kOutput, calls=%fused_computation.29 | convolution fusion | flops 409468928 | bytes 4849664 | tf_op jit(solution)/shard_map/dot_general | solution.py:88
  124.4 3.0 %fusion.94 = (f32[32,64]{1,0:T(8,128)S(1)}, f32[32,64,256]{2,1,0:T(8,128)S(1)}) fusion(f32[32,64,256]{2,1,0:T(8,128)} %fusion.13, bf16[2,256,256]{2,1,0:T(8,128)(2,1)S(1)} %copy-done.1, bf16[32,64,256]{2,1,0:T(8,128)(2,1)} %copy-done, f32[32,256]{1,0:T(8,128)S(1)} %fusion.58, f32[64]{0:T(128)S(1)} %maximum_rsqrt_fusion), kind=kOutput, calls=%fused_computation.129 | convolution fusion | flops 339216384 | bytes 6464000 | tf_op jit(solution)/shard_map/dot_general | solution.py:89
  127.4 0.6 multiply_reduce_fusion
  128.1 0.5 copy-done.3
  128.6 4.6 %select_convert_fusion = bf16[32,64,256]{2,1,0:T(8,128)(2,1)} fusion(f32[32,64,256]{2,1,0:T(8,128)S(1)} %get-tuple-element.22, f32[256]{0:T(256)S(1)} %bitcast.144, f32[32,64]{1,0:T(8,128)S(1)} %add_sqrt_fusion, f32[32,64]{1,0:T(8,128)S(1)} %broadcast_multiply_fusion, pred[32,64]{1,0:T(8,128)(4,1)S(1)} %compare_and_fusion, ...), kind=kOutput, calls=%fused_computation.14 | convolution fusion | flops 2157969408 | bytes 6363136 | tf_op jit(solution)/shard_map/dot_general | solution.py:101
  (32 shorter events, 0.4 us)
Async XLA Ops:
  0.7 45.1 %copy-start.2 = (f32[2,256]{1,0:T(2,128)S(1)}, f32[2,256]{1,0:T(2,128)}, u32[]{:S(2)}) copy-start(f32[2,256]{1,0:T(2,128)} %param.11) | copy-start | bytes 6148
  2.4 57.1 %collective-permute-start.1 = (bf16[32,32,256]{2,1,0:T(8,128)(2,1)S(1)}, bf16[32,32,256]{2,1,0:T(8,128)(2,1)S(1)}, u32[]{:S(2)}, u32[]{:S(2)}) collective-permute-start(bf16[32,32,256]{2,1,0:T(8,128)(2,1)S(1)} %get-tuple-element.14), channel_id=1, source_target_pairs={{8,0},{16,8},{24,16},{32,24},{40,32},{48,40},{56,48},{64,56},{72,6... | collective-permute-start | bytes 1572872 | tf_op jit(solution)/shard_map/ppermute | solution.py:40
  13.6 45.9 %collective-permute-start = (bf16[32,32,256]{2,1,0:T(8,128)(2,1)S(1)}, bf16[32,32,256]{2,1,0:T(8,128)(2,1)}, u32[]{:S(2)}, u32[]{:S(2)}) collective-permute-start(bf16[32,32,256]{2,1,0:T(8,128)(2,1)S(1)} %get-tuple-element.13), channel_id=1, source_target_pairs={{0,8},{8,16},{16,24},{24,32},{32,40},{40,48},{48,56},{56,64},{64,7... | collective-permute-start | bytes 1572872 | tf_op jit(solution)/shard_map/ppermute | solution.py:37
  59.5 2.0 %copy-start.4 = (bf16[2,256,256]{2,1,0:T(8,128)(2,1)S(1)}, bf16[2,256,256]{2,1,0:T(8,128)(2,1)}, u32[]{:S(2)}) copy-start(bf16[2,256,256]{2,1,0:T(8,128)(2,1)} %param.9) | copy-start | bytes 786436
  61.4 3.2 %copy-start.1 = (bf16[2,256,256]{2,1,0:T(8,128)(2,1)S(1)}, bf16[2,256,256]{2,1,0:T(8,128)(2,1)}, u32[]{:S(2)}) copy-start(bf16[2,256,256]{2,1,0:T(8,128)(2,1)} %param.10) | copy-start | bytes 786436
  71.7 49.6 %copy-start = (bf16[32,64,256]{2,1,0:T(8,128)(2,1)}, bf16[32,64,256]{2,1,0:T(8,128)(2,1)S(1)}, u32[]{:S(2)}) copy-start(bf16[32,64,256]{2,1,0:T(8,128)(2,1)S(1)} %get-tuple-element.20) | copy-start | bytes 3145732
  71.8 47.8 %collective-permute-start.3 = (bf16[32,32,256]{2,1,0:T(8,128)(2,1)S(1)}, bf16[32,32,256]{2,1,0:T(8,128)(2,1)S(1)}, u32[]{:S(2)}, u32[]{:S(2)}) collective-permute-start(bf16[32,32,256]{2,1,0:T(8,128)(2,1)S(1)} %get-tuple-element.12), channel_id=1, source_target_pairs={{8,0},{16,8},{24,16},{32,24},{40,32},{48,40},{56,48},{64,56},{72,6... | collective-permute-start | bytes 1572872 | tf_op jit(solution)/shard_map/ppermute | solution.py:40
  73.7 45.9 %collective-permute-start.2 = (bf16[32,32,256]{2,1,0:T(8,128)(2,1)S(1)}, bf16[32,32,256]{2,1,0:T(8,128)(2,1)S(1)}, u32[]{:S(2)}, u32[]{:S(2)}) collective-permute-start(bf16[32,32,256]{2,1,0:T(8,128)(2,1)S(1)} %get-tuple-element.11), channel_id=1, source_target_pairs={{0,8},{8,16},{16,24},{24,32},{32,40},{40,48},{48,56},{56,64},{64,7... | collective-permute-start | bytes 1572872 | tf_op jit(solution)/shard_map/ppermute | solution.py:37
  119.6 1.7 %copy-start.5 = (bf16[2,256,256]{2,1,0:T(8,128)(2,1)S(1)}, bf16[2,256,256]{2,1,0:T(8,128)(2,1)}, u32[]{:S(2)}) copy-start(bf16[2,256,256]{2,1,0:T(8,128)(2,1)} %param.9) | copy-start | bytes 786436
  127.4 1.2 copy-start.3
where the time goes:
time: 134 us; the launch traced here: 133 us
  blocking collectives  87.1 us (65%)
  matrix products  23.8 us (18%)
  starting transfers between devices  17.4 us (13%)
  other arithmetic  3.85 us (3%)
    all_gather x6, blocking collectives, carried_in(): pieces = lax.all_gather(total, axis)  87.1 us
    ppermute x2, starting transfers between devices, with_halo(): lax.ppermute(lax.slice_in_dim(block, 0, width, axis=dim), axis, backward)  13.1 us
    dot_general x2, matrix products, per_device(): jnp.dot(hidden, w_down[layer_index], preferred_element_type=jnp.float32)  8.47 us
    dot_general x2, matrix products, per_device(): jnp.dot(mixed_rows, w_mix[layer_index], preferred_element_type=jnp.float32)  6.34 us
    dot_general x2, matrix products, per_device(): jnp.dot(context, w_context[layer_index], preferred_element_type=jnp.float32)  5.45 us
    ppermute x2, starting transfers between devices, with_halo(): lax.ppermute(lax.slice_in_dim(block, block.shape[dim] - width, None, axis...  4.33 us
    dot_general x2, matrix products, per_device(): jnp.einsum('utd,usd->uts', center, extended, preferred_element_type=jnp.f...  3.56 us
  transfers between devices with their start and end apart: 4, of which 0 were waited for; matrix products, arithmetic and copies ran while one was open for 0% of the time, Pallas kernels for 0%

commit v1 on v0

v1 whole, which is shorter than its diff:
```python
import functools

import jax
import jax.numpy as jnp
from jax import lax
from jax.experimental import pallas as pl
from jax.experimental.pallas import tpu as pltpu
from jax.sharding import Mesh
from jax.sharding import PartitionSpec as P

D = 256
HALF = 32
LAYERS = 2
TM = ("tm_0", "tm_1", "tm_2")
ROWS = 2 * HALF
WIDE = 2 * ROWS
STEP = 16
PIECE = 4

BF16 = jnp.bfloat16
F32 = jnp.float32
VMEM = pl.BlockSpec(memory_space=pltpu.VMEM)
SMEM = pl.BlockSpec(memory_space=pltpu.SMEM)
ANY = pl.BlockSpec(memory_space=pl.ANY)
HBM = pl.BlockSpec(memory_space=pltpu.HBM)
LIMIT = pltpu.CompilerParams(vmem_limit_bytes=16 << 20)


def in_hbm(x):
    return pltpu.with_memory_space_constraint(x, pltpu.HBM)


def first_position():
    y, z, c = (lax.axis_index(a) for a in TM)
    nz, nc = (lax.axis_size(a) for a in TM[1:])
    return ((y * nz + z) * nc + c) * ROWS


def scale_rows(first_pos):
    t = lax.broadcasted_iota(jnp.int32, (ROWS, D), 0)
    return t, lax.rsqrt((first_pos + t + 1).astype(F32))


def projected(sums, weight):
    coarse = sums.astype(BF16)
    fine = (sums - coarse.astype(F32)).astype(BF16)
    return jnp.dot(coarse, weight, preferred_element_type=F32) + jnp.dot(
        fine, weight, preferred_element_type=F32
    )


def pre_kernel(
    events_ref, lengths_ref, w_ref, head_ref, tail_ref, totals_ref, buf, lens, w, sums, sems, own_sems
):
    users = head_ref.shape[0]
    blocks = sems.shape[0]
    size = users // blocks
    get_lengths = pltpu.make_async_copy(lengths_ref, lens, own_sems.at[0])
    get_w = pltpu.make_async_copy(w_ref.at[0], w, own_sems.at[1])
    get_lengths.start()

    def fetch(i):
        part = pl.ds(i * size, size)
        return pltpu.make_async_copy(events_ref.at[part], buf.at[part], sems.at[i])

    for i in range(blocks):
        fetch(i).start()
    get_w.start()
    first_pos = first_position()
    t = lax.broadcasted_iota(jnp.int32, (ROWS, D), 0)
    get_lengths.wait()
    for i in range(blocks):
        fetch(i).wait()
        rows = []
        for u in range(i * size, (i + 1) * size):
            state = jnp.where(t < lens[u] - first_pos, buf[u].astype(F32), 0.0)
            rows.append(jnp.sum(state, axis=0, keepdims=True))
            state = state.astype(BF16)
            head_ref[u] = state[:HALF]
            tail_ref[u] = state[HALF:]
        sums[i * size : (i + 1) * size] = jnp.concatenate(rows, axis=0)
    get_w.wait()
    totals = projected(sums[...], w[...]).astype(BF16)
    for k in range(totals_ref.shape[0]):
        totals_ref[k] = totals


def pre(events, lengths, w_context, copies):
    users = events.shape[0]
    half = jax.ShapeDtypeStruct((users, HALF, D), BF16)
    return pl.pallas_call(
        pre_kernel,
        in_specs=[HBM, HBM, HBM],
        out_specs=[VMEM, VMEM, VMEM],
        out_shape=[half, half, jax.ShapeDtypeStruct((copies, users, D), BF16)],
        scratch_shapes=[
            pltpu.VMEM(events.shape, BF16),
            pltpu.SMEM(lengths.shape, jnp.int32),
            pltpu.VMEM((D, D), BF16),
            pltpu.VMEM((users, D), F32),
            pltpu.SemaphoreType.DMA((4,)),
            pltpu.SemaphoreType.DMA((2,)),
        ],
        compiler_params=LIMIT,
        cost_estimate=pl.CostEstimate(
            flops=2 * events.size, bytes_accessed=4 * events.size, transcendentals=0
        ),
        name="pre",
    )(events, lengths, w_context)


def mix_kernel(layer, head, tail, low_ref, high_ref, w_mix, w_context, out, *scratch):
    low, high, tri, w, base, sems, side_sems, out_sems = scratch
    users = head.shape[0]
    gets = [
        pltpu.make_async_copy(x.at[layer], w.at[k], sems.at[k])
        for k, x in enumerate((w_mix, w_context))
    ]
    for get in gets:
        get.start()

    def sides(i):
        part = pl.ds(i * STEP, STEP)
        return [
            pltpu.make_async_copy(low_ref.at[part], low.at[part], side_sems.at[2 * i]),
            pltpu.make_async_copy(high_ref.at[part], high.at[part], side_sems.at[2 * i + 1]),
        ]

    for i in range(users // STEP):
        for get in sides(i):
            get.start()
    _, scale = scale_rows(first_position())
    r = lax.broadcasted_iota(jnp.int32, (D, D), 0)
    c = lax.broadcasted_iota(jnp.int32, (D, D), 1)
    tri[...] = jnp.where((c <= r) & (c >= r - lax.rem(r, ROWS)), 1.0, 0.0).astype(BF16)
    r = lax.broadcasted_iota(jnp.int32, (2 * ROWS, 2 * WIDE), 0)
    s = lax.broadcasted_iota(jnp.int32, (2 * ROWS, 2 * WIDE), 1)
    first = r + jnp.where(r >= ROWS, WIDE - ROWS, 0)
    band = (s >= first) & (s <= first + 2 * HALF)
    for get in gets:
        get.wait()

    def store(i):
        part = pl.ds(i * PIECE, PIECE)
        return pltpu.make_async_copy(base.at[part], out.at[part], out_sems.at[i])

    def body(i, carry):
        b = i * STEP
        for get in sides(i):
            get.wait()
        owns, exts, scores = [], [], []
        for u in range(0, STEP, 2):
            u = b + u
            own = [head[u], tail[u], head[u + 1], tail[u + 1]]
            ext = jnp.concatenate(
                [low[u], own[0], own[1], high[u], low[u + 1], own[2], own[3], high[u + 1]], axis=0
            )
            own = jnp.concatenate(own, axis=0)
            owns.append(own)
            exts.append(ext)
            scores.append(
                lax.dot_general(own, ext, (((1,), (1,)), ((), ())), preferred_element_type=F32)
            )
        weights = [jnp.where(band, x * (1.0 / D), 0.0).astype(BF16) for x in scores]
        mixed = [
            jnp.dot(w, e, preferred_element_type=F32).astype(BF16) for w, e in zip(weights, exts)
        ]
        own = jnp.concatenate(owns, axis=0)
        running = [
            jnp.dot(tri[...], own[k : k + D], preferred_element_type=F32).astype(BF16)
            for k in range(0, STEP * ROWS, D)
        ]
        summed = own.astype(F32) + jnp.dot(
            jnp.concatenate(mixed, axis=0), w[0], preferred_element_type=F32
        )
        local = jnp.dot(jnp.concatenate(running, axis=0), w[1], preferred_element_type=F32)
        for k in range(STEP):
            part = slice(k * ROWS, (k + 1) * ROWS)
            base[b + k] = summed[part] + local[part] * scale
            if k % PIECE == PIECE - 1:
                store(i * (STEP // PIECE) + k // PIECE).start()
        return carry

    lax.fori_loop(0, users // STEP, body, 0)
    for i in range(users // PIECE):
        store(i).wait()


def mix(layer, head, tail, low, high, w_mix, w_context):
    users = head.shape[0]
    return pl.pallas_call(
        functools.partial(mix_kernel, layer),
        in_specs=[VMEM] * 2 + [ANY] * 2 + [HBM] * 2,
        out_specs=HBM,
        out_shape=pltpu.HBM((users, ROWS, D), F32),
        scratch_shapes=[
            pltpu.VMEM((users, HALF, D), BF16),
            pltpu.VMEM((users, HALF, D), BF16),
            pltpu.VMEM((D, D), BF16),
            pltpu.VMEM((2, D, D), BF16),
            pltpu.VMEM((users, ROWS, D), F32),
            pltpu.SemaphoreType.DMA((2,)),
            pltpu.SemaphoreType.DMA((2 * (users // STEP),)),
            pltpu.SemaphoreType.DMA((users // PIECE,)),
        ],
        compiler_params=LIMIT,
        cost_estimate=pl.CostEstimate(
            flops=2 * users * ROWS * D * (2 * 2 * WIDE + 3 * D),
            bytes_accessed=8 * users * ROWS * D,
            transcendentals=0,
        ),
        name="mix",
    )(head, tail, low, high, w_mix, w_context)


def post_kernel(layer, last, lengths, base_ref, parts, gains, w_up, w_down, *refs):
    *refs, base, base_sems = refs
    users = base.shape[0]

    def fetch(i):
        part = pl.ds(i * PIECE, PIECE)
        return pltpu.make_async_copy(base_ref.at[part], base.at[part], base_sems.at[i])

    for i in range(users // PIECE):
        fetch(i).start()
    if last:
        out_ref, out_buf, add, sems = refs
    else:
        w_ref, head_ref, tail_ref, totals_ref, add, sums, w, sem = refs
        get_w = pltpu.make_async_copy(w_ref.at[layer + 1], w, sem)
        get_w.start()
    first_pos = first_position()
    t, scale = scale_rows(first_pos)
    add[...] = jnp.sum(parts[...].astype(F32), axis=0)
    gain = gains[layer : layer + 1]

    def store(i):
        part = pl.ds(i * PIECE, PIECE)
        return pltpu.make_async_copy(out_buf.at[part], out_ref.at[part], sems.at[i])

    def body(i, carry):
        b = pl.multiple_of(i * STEP, STEP)
        for k in range(STEP // PIECE):
            fetch(i * (STEP // PIECE) + k).wait()
        more = add[pl.ds(b, STEP)]
        summed = jnp.concatenate(
            [base[b + k] + more[k : k + 1] * scale for k in range(STEP)], axis=0
        )
        mean = jnp.mean(summed, axis=-1, keepdims=True)
        centered = summed - mean
        var = jnp.mean(centered * centered, axis=-1, keepdims=True)
        normed = (centered * lax.rsqrt(var + 1e-05) * gain).astype(BF16)
        hidden = jnp.dot(normed, w_up[layer], preferred_element_type=F32)
        hidden = jnp.maximum(hidden, 0.0).astype(BF16)
        result = normed.astype(F32) + jnp.dot(hidden, w_down[layer], preferred_element_type=F32)
        rows = []
        for k in range(STEP):
            u = b + k
            state = jnp.where(
                t < lengths[u] - first_pos, result[k * ROWS : (k + 1) * ROWS], 0.0
            ).astype(BF16)
            if last:
                out_buf[u] = state
                if k % PIECE == PIECE - 1:
                    store(i * (STEP // PIECE) + k // PIECE).start()
            else:
                head_ref[u] = state[:HALF]
                tail_ref[u] = state[HALF:]
                rows.append(jnp.sum(state.astype(F32), axis=0, keepdims=True))
        if not last:
            sums[pl.ds(b, STEP)] = jnp.concatenate(rows, axis=0)
        return carry

    lax.fori_loop(0, users // STEP, body, 0)
    if last:
        for i in range(users // PIECE):
            store(i).wait()
    else:
        get_w.wait()
        totals = projected(sums[...], w[...]).astype(BF16)
        for k in range(totals_ref.shape[0]):
            totals_ref[k] = totals


def post(layer, last, copies, lengths, base, parts, w_context, gains, w_up, w_down):
    users = base.shape[0]
    in_specs = [SMEM, HBM] + [VMEM] * 4
    args = (lengths, in_hbm(base), parts, gains, w_up, w_down)
    if last:
        out_specs = HBM
        out_shape = jax.ShapeDtypeStruct((users, ROWS, D), BF16)
        scratch = [
            pltpu.VMEM((users, ROWS, D), BF16),
            pltpu.VMEM((users, D), F32),
            pltpu.SemaphoreType.DMA((users // PIECE,)),
        ]
    else:
        half = jax.ShapeDtypeStruct((users, HALF, D), BF16)
        in_specs.append(HBM)
        args += (w_context,)
        out_specs = [VMEM, VMEM, VMEM]
        out_shape = [half, half, jax.ShapeDtypeStruct((copies, users, D), BF16)]
        scratch = [
            pltpu.VMEM((users, D), F32),
            pltpu.VMEM((users, D), F32),
            pltpu.VMEM((D, D), BF16),
            pltpu.SemaphoreType.DMA,
        ]
    scratch += [pltpu.VMEM((users, ROWS, D), F32), pltpu.SemaphoreType.DMA((users // PIECE,))]
    return pl.pallas_call(
        functools.partial(post_kernel, layer, last),
        in_specs=in_specs,
        out_specs=out_specs,
        out_shape=out_shape,
        scratch_shapes=scratch,
        compiler_params=LIMIT,
        cost_estimate=pl.CostEstimate(
            flops=4 * users * ROWS * D * w_up.shape[2],
            bytes_accessed=6 * users * ROWS * D,
            transcendentals=0,
        ),
        name="post",
    )(*args)


def messages(totals):
    y, z, c = (lax.axis_index(a) for a in TM)
    ny, nz, nc = (lax.axis_size(a) for a in TM)
    got = lax.all_to_all(totals, ("tm_0", "tm_2"), 0, 0, tiled=True)
    got = got.reshape(ny, nc, *got.shape[1:]).astype(F32)
    k = jnp.arange(ny)[:, None, None, None]
    j = jnp.arange(nc)[None, :, None, None]
    base = jnp.sum(jnp.where(k < y, got, 0.0), axis=(0, 1))
    row = jnp.sum(jnp.where(k == y, got, 0.0), axis=(0, 1))
    own = jnp.sum(jnp.where((k == y) & (j < c), got, 0.0), axis=(0, 1))
    to = jnp.arange(nz)[:, None, None]
    sent = base[None] + jnp.where(to > z, row[None], jnp.where(to == z, own[None], 0.0))
    return sent.astype(BF16)


def halos(head, tail):
    n = lax.axis_size(TM)
    up = [(i, i + 1) for i in range(n - 1)]
    down = [(i + 1, i) for i in range(n - 1)]
    return lax.ppermute(tail, TM, up), lax.ppermute(head, TM, down)


def per_device(events, lengths, w_mix, w_context, gains, w_up, w_down):
    copies = lax.axis_size(("tm_0", "tm_2"))
    w_mix, w_context = in_hbm(w_mix), in_hbm(w_context)
    head, tail, totals = pre(in_hbm(events), in_hbm(lengths), w_context, copies)
    for layer in range(LAYERS):
        last = layer == LAYERS - 1
        low, high = halos(head, tail)
        parts = lax.all_to_all(messages(totals), "tm_1", 0, 0, tiled=True)
        base = mix(layer, head, tail, low, high, w_mix, w_context)
        out = post(layer, last, copies, lengths, base, parts, w_context, gains, w_up, w_down)
        if last:
            return out
        head, tail, totals = out


def solution(mesh):
    torus = Mesh(
        mesh.devices.reshape(4, 8, 2, mesh.shape["user"]), ("tm_0", "tm_1", "tm_2", "user")
    )
    return jax.shard_map(
        per_device,
        mesh=torus,
        in_specs=(P("user", TM, None), P("user"), P(), P(), P(), P(), P()),
        out_specs=P("user", TM, None),
        check_vma=False,
    )
```

time: 134 us -> 74.3 us (0.55)
  blocking collectives: 87.1 us -> 0 us
  matrix products: 23.8 us -> 0 us
  Pallas kernels: 0 us -> 22.7 us
  starting transfers between devices: 17.4 us -> 35 us
  waiting for transfers between devices: 0.01 us -> 13.3 us
  other arithmetic: 3.85 us -> 1.79 us
    all_gather x6 -> x0, blocking collectives: 87.1 us -> none  [carried_in(): pieces = lax.all_gather(total, axis)]
    dot_general x8 -> x0, matrix products: 23.8 us -> none  [the longest x2 8.47 us: per_device(): jnp.dot(hidden, w_down[layer_index], preferred_element_type=jnp.float32)]
    pallas_call x0 -> x5, Pallas kernels: none -> 22.7 us  [the longest x2 12 us: post(): pl.pallas_call(functools.partial(post_kernel, layer, last), in_specs=in_s...]
    all_to_all x0 -> x4, starting transfers between devices: none -> 18.1 us  [the longest x2 11.3 us: messages(): got = lax.all_to_all(totals, ('tm_0', 'tm_2'), 0, 0, tiled=True)]
    ppermute x4, waiting for transfers between devices: 0.01 us -> 13.3 us  [halos(): return (lax.ppermute(tail, TM, up), lax.ppermute(head, TM, down))]
    reduce_sum x3 -> x2, other arithmetic: 2.86 us -> 0.24 us  [messages(): base = jnp.sum(jnp.where(k < y, got, 0.0), axis=(0, 1))]
    convert_element_type x0 -> x2, other arithmetic: none -> 1.52 us  [messages(): return sent.astype(BF16)]
  transfers between devices with their start and end apart: 4 -> 8, of which waited for: 0 -> 2; matrix products, arithmetic and copies ran while one was open for 0% -> 3% of each run, Pallas kernels for 0% -> 12%
where the time goes in v1:
time: 74.3 us; the launch traced here: 73.5 us
  starting transfers between devices  35 us (47%)
  Pallas kernels  22.7 us (31%)
  waiting for transfers between devices  13.3 us (18%)
  other arithmetic  1.79 us (2%)
    ppermute x4, starting transfers between devices, halos(): return (lax.ppermute(tail, TM, up), lax.ppermute(head, TM, down))  16.9 us
    ppermute x4, waiting for transfers between devices, halos(): return (lax.ppermute(tail, TM, up), lax.ppermute(head, TM, down))  13.3 us
    pallas_call x2, Pallas kernels, post(): pl.pallas_call(functools.partial(post_kernel, layer, last), in_specs=in_s...  12 us
    all_to_all x2, starting transfers between devices, messages(): got = lax.all_to_all(totals, ('tm_0', 'tm_2'), 0, 0, tiled=True)  11.3 us
    pallas_call x2, Pallas kernels, mix(): pl.pallas_call(functools.partial(mix_kernel, layer), in_specs=[VMEM] * 2...  8.49 us
    all_to_all x2, starting transfers between devices, per_device(): parts = lax.all_to_all(messages(totals), 'tm_1', 0, 0, tiled=True)  6.74 us
    pallas_call x1, Pallas kernels, pre(): pl.pallas_call(pre_kernel, in_specs=[HBM, HBM, HBM], out_specs=[VMEM, VME...  2.16 us
    convert_element_type x2, other arithmetic, messages(): return sent.astype(BF16)  1.52 us
  transfers between devices with their start and end apart: 8, of which 2 were waited for; matrix products, arithmetic and copies ran while one was open for 3% of the time, Pallas kernels for 12%

profile of v1, /device:TPU:56, one launch (start us, length us, event | category | flops | bytes accessed | tf_op | source)
XLA Modules:
  0.0 73.5 jit_solution(13462173648607216527)
XLA Ops:
  0.0 2.2 %pre.1 = (bf16[32,32,256]{2,1,0:T(8,128)(2,1)S(1)}, bf16[32,32,256]{2,1,0:T(8,128)(2,1)S(1)}, bf16[8,32,256]{2,1,0:T(8,128)(2,1)}) custom-call(bf16[32,64,256]{2,1,0:T(8,128)(2,1)} %events_ref.1, s32[32]{0:T(128)} %lengths.3, bf16[2,256,256]{2,1,0:T(8,128)(2,1)} %w_context.3), custom_call_target="tpu_custom_call" | custom-call | flops 1048576 | bytes 2097152 | tf_op jit(solution)/shard_map/pre/pallas_call | solution.py:91
  2.2 6.2 %all-to-all-start = ((bf16[8,32,256]{2,1,0:T(8,128)(2,1)}), bf16[8,32,256]{2,1,0:T(8,128)(2,1)S(1)}, u32[]{:S(2)}, u32[]{:S(2)}) async-start(bf16[8,32,256]{2,1,0:T(8,128)(2,1)} %get-tuple-element.13), calls=%async_computation | async-start | bytes 262144 | tf_op jit(solution)/shard_map/all_to_all | solution.py:329
  8.4 10.7 %collective-permute-start.1 = (bf16[32,32,256]{2,1,0:T(8,128)(2,1)S(1)}, bf16[32,32,256]{2,1,0:T(8,128)(2,1)}, u32[]{:S(2)}, u32[]{:S(2)}) collective-permute-start(bf16[32,32,256]{2,1,0:T(8,128)(2,1)S(1)} %get-tuple-element.11.head), channel_id=1, source_target_pairs={{8,0},{16,8},{24,16},{32,24},{40,32},{48,40},{56,48},{64,56},{72,6... | collective-permute-start | bytes 1572872 | tf_op jit(solution)/shard_map/ppermute | solution.py:345
  19.1 1.9 %collective-permute-start = (bf16[32,32,256]{2,1,0:T(8,128)(2,1)S(1)}, bf16[32,32,256]{2,1,0:T(8,128)(2,1)}, u32[]{:S(2)}, u32[]{:S(2)}) collective-permute-start(bf16[32,32,256]{2,1,0:T(8,128)(2,1)S(1)} %get-tuple-element.12.tail), channel_id=1, source_target_pairs={{0,8},{8,16},{16,24},{24,32},{32,40},{40,48},{48,56},{56,64},{64,7... | collective-permute-start | bytes 1572872 | tf_op jit(solution)/shard_map/ppermute | solution.py:345
  21.1 0.1 and.29
  21.2 0.1 broadcast_in_dim.116
  21.2 0.1 broadcast_in_dim.117
  21.3 0.1 broadcast_in_dim.111
  21.4 0.1 broadcast_in_dim.112
  21.5 0.1 fusion
  21.6 0.8 %add_convert_fusion.1 = bf16[8,32,256]{2,1,0:T(8,128)(2,1)} fusion(f32[32,256]{1,0:T(8,128)S(1)} %get-tuple-element.22, f32[32,256]{1,0:T(8,128)S(1)} %get-tuple-element.21, f32[32,256]{1,0:T(8,128)S(1)} %get-tuple-element.20, pred[8]{0:T(512)(128)(4,1)S(1)} %get-tuple-element.25, pred[8]{0:T(512)(128)(4,1)S(1)} %get-tuple-element.26), kind=kLoop, calls=%fused_computation.13 | loop fusion | flops 262144 | bytes 229392 | tf_op jit(solution)/shard_map/convert_element_type | solution.py:338
  22.4 3.4 %all-to-all-start.1 = ((bf16[8,32,256]{2,1,0:T(8,128)(2,1)}), bf16[8,32,256]{2,1,0:T(8,128)(2,1)S(1)}, u32[]{:S(2)}, u32[]{:S(2)}) async-start(bf16[8,32,256]{2,1,0:T(8,128)(2,1)} %add_convert_fusion.1), calls=%async_computation.1 | async-start | bytes 262144 | tf_op jit(solution)/shard_map/all_to_all | solution.py:355
  25.8 7.1 %collective-permute-done.low_ref = bf16[32,32,256]{2,1,0:T(8,128)(2,1)} collective-permute-done((bf16[32,32,256]{2,1,0:T(8,128)(2,1)S(1)}, bf16[32,32,256]{2,1,0:T(8,128)(2,1)}, u32[]{:S(2)}, u32[]{:S(2)}) %collective-permute-start) | collective-permute-done | bytes 524320 | tf_op jit(solution)/shard_map/ppermute | solution.py:345
  33.0 4.2 %mix.2.base_ref = f32[32,64,256]{2,1,0:T(8,128)} custom-call(bf16[32,32,256]{2,1,0:T(8,128)(2,1)S(1)} %get-tuple-element.11.head, bf16[32,32,256]{2,1,0:T(8,128)(2,1)S(1)} %get-tuple-element.12.tail, bf16[32,32,256]{2,1,0:T(8,128)(2,1)} %collective-permute-done.low_ref, bf16[32,32,256]{2,1,0:T(8,128)(2,1)} %collective-permute-done.1.high_ref, ...), custom_call_target="tpu_custom_call" | custom-call | flops 1342177280 | bytes 4194304 | tf_op jit(solution)/shard_map/mix/pallas_call | solution.py:191
  37.3 6.1 %post.2 = (bf16[32,32,256]{2,1,0:T(8,128)(2,1)S(1)}, bf16[32,32,256]{2,1,0:T(8,128)(2,1)S(1)}, bf16[8,32,256]{2,1,0:T(8,128)(2,1)}) custom-call(s32[32]{0:T(128)S(1)} %copy-done, f32[32,64,256]{2,1,0:T(8,128)} %mix.2.base_ref, bf16[8,32,256]{2,1,0:T(8,128)(2,1)S(1)} %all-to-all-done.1.parts, f32[2,256]{1,0:T(2,128)S(1)} %copy-done.3, ...), custom_call_target="tpu_custom_call" | custom-call | flops 2147483648 | bytes 3145728 | tf_op jit(solution)/shard_map/post/pallas_call | solution.py:310
  43.4 5.1 %all-to-all-start.2 = ((bf16[8,32,256]{2,1,0:T(8,128)(2,1)}), bf16[8,32,256]{2,1,0:T(8,128)(2,1)S(1)}, u32[]{:S(2)}, u32[]{:S(2)}) async-start(bf16[8,32,256]{2,1,0:T(8,128)(2,1)} %get-tuple-element.16), calls=%async_computation.2 | async-start | bytes 262144 | tf_op jit(solution)/shard_map/all_to_all | solution.py:329
  48.5 1.9 %collective-permute-start.3 = (bf16[32,32,256]{2,1,0:T(8,128)(2,1)S(1)}, bf16[32,32,256]{2,1,0:T(8,128)(2,1)}, u32[]{:S(2)}, u32[]{:S(2)}) collective-permute-start(bf16[32,32,256]{2,1,0:T(8,128)(2,1)S(1)} %get-tuple-element.14.head), channel_id=1, source_target_pairs={{8,0},{16,8},{24,16},{32,24},{40,32},{48,40},{56,48},{64,56},{72,6... | collective-permute-start | bytes 1572872 | tf_op jit(solution)/shard_map/ppermute | solution.py:345
  50.4 2.4 %collective-permute-start.2 = (bf16[32,32,256]{2,1,0:T(8,128)(2,1)S(1)}, bf16[32,32,256]{2,1,0:T(8,128)(2,1)}, u32[]{:S(2)}, u32[]{:S(2)}) collective-permute-start(bf16[32,32,256]{2,1,0:T(8,128)(2,1)S(1)} %get-tuple-element.15.tail), channel_id=1, source_target_pairs={{0,8},{8,16},{16,24},{24,32},{32,40},{40,48},{48,56},{56,64},{64,7... | collective-permute-start | bytes 1572872 | tf_op jit(solution)/shard_map/ppermute | solution.py:345
  52.9 0.1 fusion.3
  53.0 0.8 %add_convert_fusion = bf16[8,32,256]{2,1,0:T(8,128)(2,1)} fusion(f32[32,256]{1,0:T(8,128)S(1)} %get-tuple-element.19, f32[32,256]{1,0:T(8,128)S(1)} %get-tuple-element.18, f32[32,256]{1,0:T(8,128)S(1)} %get-tuple-element.17, pred[8]{0:T(512)(128)(4,1)S(1)} %get-tuple-element.25, pred[8]{0:T(512)(128)(4,1)S(1)} %get-tuple-element.26), kind=kLoop, calls=%fused_computation.12 | loop fusion | flops 262144 | bytes 229392 | tf_op jit(solution)/shard_map/convert_element_type | solution.py:338
  53.7 3.4 %all-to-all-start.3 = ((bf16[8,32,256]{2,1,0:T(8,128)(2,1)}), bf16[8,32,256]{2,1,0:T(8,128)(2,1)S(1)}, u32[]{:S(2)}, u32[]{:S(2)}) async-start(bf16[8,32,256]{2,1,0:T(8,128)(2,1)} %add_convert_fusion), calls=%async_computation.3 | async-start | bytes 262144 | tf_op jit(solution)/shard_map/all_to_all | solution.py:355
  57.1 6.2 %collective-permute-done.2.low_ref = bf16[32,32,256]{2,1,0:T(8,128)(2,1)} collective-permute-done((bf16[32,32,256]{2,1,0:T(8,128)(2,1)S(1)}, bf16[32,32,256]{2,1,0:T(8,128)(2,1)}, u32[]{:S(2)}, u32[]{:S(2)}) %collective-permute-start.2) | collective-permute-done | bytes 524320 | tf_op jit(solution)/shard_map/ppermute | solution.py:345
  63.3 4.2 %mix.3.base_ref = f32[32,64,256]{2,1,0:T(8,128)} custom-call(bf16[32,32,256]{2,1,0:T(8,128)(2,1)S(1)} %get-tuple-element.14.head, bf16[32,32,256]{2,1,0:T(8,128)(2,1)S(1)} %get-tuple-element.15.tail, bf16[32,32,256]{2,1,0:T(8,128)(2,1)} %collective-permute-done.2.low_ref, bf16[32,32,256]{2,1,0:T(8,128)(2,1)} %collective-permute-done.3.high_ref, ...), custom_call_target="tpu_custom_call" | custom-call | flops 1342177280 | bytes 4194304 | tf_op jit(solution)/shard_map/mix/pallas_call | solution.py:191
  67.6 5.9 %post.3 = bf16[32,64,256]{2,1,0:T(8,128)(2,1)} custom-call(s32[32]{0:T(128)S(1)} %copy-done, f32[32,64,256]{2,1,0:T(8,128)} %mix.3.base_ref, bf16[8,32,256]{2,1,0:T(8,128)(2,1)S(1)} %all-to-all-done.3.parts, f32[2,256]{1,0:T(2,128)S(1)} %copy-done.3, bf16[2,256,1024]{2,1,0:T(8,128)(2,1)S(1)} %copy-done.1, bf16[2,1024,256]{2,1,0:T(8,128)(2,1)S(1)} %copy-done.2), custom_call_target="tpu_custom_call" | custom-call | flops 2147483648 | bytes 3145728 | tf_op jit(solution)/shard_map/post/pallas_call | solution.py:310
  (19 shorter events, 0.1 us)
Async XLA Ops:
  2.2 19.3 %all-to-all-start = ((bf16[8,32,256]{2,1,0:T(8,128)(2,1)}), bf16[8,32,256]{2,1,0:T(8,128)(2,1)S(1)}, u32[]{:S(2)}, u32[]{:S(2)}) async-start(bf16[8,32,256]{2,1,0:T(8,128)(2,1)} %get-tuple-element.13), calls=%async_computation | async-start | bytes 262144 | tf_op jit(solution)/shard_map/all_to_all | solution.py:329
  8.4 17.4 %collective-permute-start.1 = (bf16[32,32,256]{2,1,0:T(8,128)(2,1)S(1)}, bf16[32,32,256]{2,1,0:T(8,128)(2,1)}, u32[]{:S(2)}, u32[]{:S(2)}) collective-permute-start(bf16[32,32,256]{2,1,0:T(8,128)(2,1)S(1)} %get-tuple-element.11.head), channel_id=1, source_target_pairs={{8,0},{16,8},{24,16},{32,24},{40,32},{48,40},{56,48},{64,56},{72,6... | collective-permute-start | bytes 1572872 | tf_op jit(solution)/shard_map/ppermute | solution.py:345
  19.1 13.9 %collective-permute-start = (bf16[32,32,256]{2,1,0:T(8,128)(2,1)S(1)}, bf16[32,32,256]{2,1,0:T(8,128)(2,1)}, u32[]{:S(2)}, u32[]{:S(2)}) collective-permute-start(bf16[32,32,256]{2,1,0:T(8,128)(2,1)S(1)} %get-tuple-element.12.tail), channel_id=1, source_target_pairs={{0,8},{8,16},{16,24},{24,32},{32,40},{40,48},{48,56},{56,64},{64,7... | collective-permute-start | bytes 1572872 | tf_op jit(solution)/shard_map/ppermute | solution.py:345
  22.4 14.8 %all-to-all-start.1 = ((bf16[8,32,256]{2,1,0:T(8,128)(2,1)}), bf16[8,32,256]{2,1,0:T(8,128)(2,1)S(1)}, u32[]{:S(2)}, u32[]{:S(2)}) async-start(bf16[8,32,256]{2,1,0:T(8,128)(2,1)} %add_convert_fusion.1), calls=%async_computation.1 | async-start | bytes 262144 | tf_op jit(solution)/shard_map/all_to_all | solution.py:355
  25.8 11.4 %copy-start = (s32[32]{0:T(128)S(1)}, s32[32]{0:T(128)}, u32[]{:S(2)}) copy-start(s32[32]{0:T(128)} %lengths.3) | copy-start | bytes 388
  25.8 11.4 %copy-start.1 = (bf16[2,256,1024]{2,1,0:T(8,128)(2,1)S(1)}, bf16[2,256,1024]{2,1,0:T(8,128)(2,1)}, u32[]{:S(2)}) copy-start(bf16[2,256,1024]{2,1,0:T(8,128)(2,1)} %w_up.3) | copy-start | bytes 3145732
  25.8 11.4 %copy-start.2 = (bf16[2,1024,256]{2,1,0:T(8,128)(2,1)S(1)}, bf16[2,1024,256]{2,1,0:T(8,128)(2,1)}, u32[]{:S(2)}) copy-start(bf16[2,1024,256]{2,1,0:T(8,128)(2,1)} %w_down.3) | copy-start | bytes 3145732
  25.8 11.4 %copy-start.3 = (f32[2,256]{1,0:T(2,128)S(1)}, f32[2,256]{1,0:T(2,128)}, u32[]{:S(2)}) copy-start(f32[2,256]{1,0:T(2,128)} %gains.3) | copy-start | bytes 6148
  43.4 9.5 %all-to-all-start.2 = ((bf16[8,32,256]{2,1,0:T(8,128)(2,1)}), bf16[8,32,256]{2,1,0:T(8,128)(2,1)S(1)}, u32[]{:S(2)}, u32[]{:S(2)}) async-start(bf16[8,32,256]{2,1,0:T(8,128)(2,1)} %get-tuple-element.16), calls=%async_computation.2 | async-start | bytes 262144 | tf_op jit(solution)/shard_map/all_to_all | solution.py:329
  48.5 8.6 %collective-permute-start.3 = (bf16[32,32,256]{2,1,0:T(8,128)(2,1)S(1)}, bf16[32,32,256]{2,1,0:T(8,128)(2,1)}, u32[]{:S(2)}, u32[]{:S(2)}) collective-permute-start(bf16[32,32,256]{2,1,0:T(8,128)(2,1)S(1)} %get-tuple-element.14.head), channel_id=1, source_target_pairs={{8,0},{16,8},{24,16},{32,24},{40,32},{48,40},{56,48},{64,56},{72,6... | collective-permute-start | bytes 1572872 | tf_op jit(solution)/shard_map/ppermute | solution.py:345
  50.4 12.9 %collective-permute-start.2 = (bf16[32,32,256]{2,1,0:T(8,128)(2,1)S(1)}, bf16[32,32,256]{2,1,0:T(8,128)(2,1)}, u32[]{:S(2)}, u32[]{:S(2)}) collective-permute-start(bf16[32,32,256]{2,1,0:T(8,128)(2,1)S(1)} %get-tuple-element.15.tail), channel_id=1, source_target_pairs={{0,8},{8,16},{16,24},{24,32},{32,40},{40,48},{48,56},{56,64},{64,7... | collective-permute-start | bytes 1572872 | tf_op jit(solution)/shard_map/ppermute | solution.py:345
  53.7 13.8 %all-to-all-start.3 = ((bf16[8,32,256]{2,1,0:T(8,128)(2,1)}), bf16[8,32,256]{2,1,0:T(8,128)(2,1)S(1)}, u32[]{:S(2)}, u32[]{:S(2)}) async-start(bf16[8,32,256]{2,1,0:T(8,128)(2,1)} %add_convert_fusion), calls=%async_computation.3 | async-start | bytes 262144 | tf_op jit(solution)/shard_map/all_to_all | solution.py:355

commit v2 on v1

--- a/solution.py
+++ b/solution.py
@@ -20,7 +20,6 @@
 BF16 = jnp.bfloat16
 F32 = jnp.float32
 VMEM = pl.BlockSpec(memory_space=pltpu.VMEM)
-SMEM = pl.BlockSpec(memory_space=pltpu.SMEM)
 ANY = pl.BlockSpec(memory_space=pl.ANY)
 HBM = pl.BlockSpec(memory_space=pltpu.HBM)
 LIMIT = pltpu.CompilerParams(vmem_limit_bytes=16 << 20)
@@ -36,8 +35,19 @@
     return ((y * nz + z) * nc + c) * ROWS
 
 
+def place(index, halves):
+    half = lax.div(index, HALF)
+    back = lax.axis_index(TM[2]) == 1
+    return jnp.where(back, halves - 1 - half, half) * HALF + lax.rem(index, HALF)
+
+
+def half_starts():
+    c = lax.axis_index(TM[2])
+    return pl.multiple_of(c * HALF, HALF), pl.multiple_of((1 - c) * HALF, HALF)
+
+
 def scale_rows(first_pos):
-    t = lax.broadcasted_iota(jnp.int32, (ROWS, D), 0)
+    t = place(lax.broadcasted_iota(jnp.int32, (ROWS, D), 0), 2)
     return t, lax.rsqrt((first_pos + t + 1).astype(F32))
 
 
@@ -50,9 +60,9 @@
 
 
 def pre_kernel(
-    events_ref, lengths_ref, w_ref, head_ref, tail_ref, totals_ref, buf, lens, w, sums, sems, own_sems
+    events_ref, lengths_ref, w_ref, outer_ref, inner_ref, totals_ref, buf, lens, w, sums, sems, own_sems
 ):
-    users = head_ref.shape[0]
+    users = outer_ref.shape[0]
     blocks = sems.shape[0]
     size = users // blocks
     get_lengths = pltpu.make_async_copy(lengths_ref, lens, own_sems.at[0])
@@ -67,17 +77,19 @@
         fetch(i).start()
     get_w.start()
     first_pos = first_position()
-    t = lax.broadcasted_iota(jnp.int32, (ROWS, D), 0)
+    t, _ = scale_rows(first_pos)
+    starts = half_starts()
     get_lengths.wait()
     for i in range(blocks):
         fetch(i).wait()
         rows = []
         for u in range(i * size, (i + 1) * size):
-            state = jnp.where(t < lens[u] - first_pos, buf[u].astype(F32), 0.0)
+            state = jnp.concatenate([buf[u, pl.ds(start, HALF)] for start in starts], axis=0)
+            state = jnp.where(t < lens[u] - first_pos, state.astype(F32), 0.0)
             rows.append(jnp.sum(state, axis=0, keepdims=True))
             state = state.astype(BF16)
-            head_ref[u] = state[:HALF]
-            tail_ref[u] = state[HALF:]
+            outer_ref[u] = state[:HALF]
+            inner_ref[u] = state[HALF:]
         sums[i * size : (i + 1) * size] = jnp.concatenate(rows, axis=0)
     get_w.wait()
     totals = projected(sums[...], w[...]).astype(BF16)
@@ -109,9 +121,9 @@
     )(events, lengths, w_context)
 
 
-def mix_kernel(layer, head, tail, low_ref, high_ref, w_mix, w_context, out, *scratch):
-    low, high, tri, w, base, sems, side_sems, out_sems = scratch
-    users = head.shape[0]
+def mix_kernel(layer, outer, inner, far_ref, near_ref, w_mix, w_context, out, *scratch):
+    far, near, tri, w, base, sems, side_sems, out_sems = scratch
+    users = outer.shape[0]
     gets = [
         pltpu.make_async_copy(x.at[layer], w.at[k], sems.at[k])
         for k, x in enumerate((w_mix, w_context))
@@ -122,8 +134,8 @@
     def sides(i):
         part = pl.ds(i * STEP, STEP)
         return [
-            pltpu.make_async_copy(low_ref.at[part], low.at[part], side_sems.at[2 * i]),
-            pltpu.make_async_copy(high_ref.at[part], high.at[part], side_sems.at[2 * i + 1]),
+            pltpu.make_async_copy(far_ref.at[part], far.at[part], side_sems.at[2 * i]),
+            pltpu.make_async_copy(near_ref.at[part], near.at[part], side_sems.at[2 * i + 1]),
         ]
 
     for i in range(users // STEP):
@@ -132,11 +144,13 @@
     _, scale = scale_rows(first_position())
     r = lax.broadcasted_iota(jnp.int32, (D, D), 0)
     c = lax.broadcasted_iota(jnp.int32, (D, D), 1)
-    tri[...] = jnp.where((c <= r) & (c >= r - lax.rem(r, ROWS)), 1.0, 0.0).astype(BF16)
+    same = lax.div(r, ROWS) == lax.div(c, ROWS)
+    earlier = place(lax.rem(c, ROWS), 2) <= place(lax.rem(r, ROWS), 2)
+    tri[...] = jnp.where(same & earlier, 1.0, 0.0).astype(BF16)
     r = lax.broadcasted_iota(jnp.int32, (2 * ROWS, 2 * WIDE), 0)
     s = lax.broadcasted_iota(jnp.int32, (2 * ROWS, 2 * WIDE), 1)
-    first = r + jnp.where(r >= ROWS, WIDE - ROWS, 0)
-    band = (s >= first) & (s <= first + 2 * HALF)
+    apart = place(lax.rem(s, WIDE), 4) - place(lax.rem(r, ROWS), 2)
+    band = (lax.div(r, ROWS) == lax.div(s, WIDE)) & (apart >= 0) & (apart <= 2 * HALF)
     for get in gets:
         get.wait()
 
@@ -151,9 +165,9 @@
         owns, exts, scores = [], [], []
         for u in range(0, STEP, 2):
             u = b + u
-            own = [head[u], tail[u], head[u + 1], tail[u + 1]]
+            own = [outer[u], inner[u], outer[u + 1], inner[u + 1]]
             ext = jnp.concatenate(
-                [low[u], own[0], own[1], high[u], low[u + 1], own[2], own[3], high[u + 1]], axis=0
+                [far[u], own[0], own[1], near[u], far[u + 1], own[2], own[3], near[u + 1]], axis=0
             )
             own = jnp.concatenate(own, axis=0)
             owns.append(own)
@@ -186,8 +200,8 @@
         store(i).wait()
 
 
-def mix(layer, head, tail, low, high, w_mix, w_context):
-    users = head.shape[0]
+def mix(layer, outer, inner, far, near, w_mix, w_context):
+    users = outer.shape[0]
     return pl.pallas_call(
         functools.partial(mix_kernel, layer),
         in_specs=[VMEM] * 2 + [ANY] * 2 + [HBM] * 2,
@@ -210,29 +224,35 @@
             transcendentals=0,
         ),
         name="mix",
-    )(head, tail, low, high, w_mix, w_context)
-
-
-def post_kernel(layer, last, lengths, base_ref, parts, gains, w_up, w_down, *refs):
-    *refs, base, base_sems = refs
+    )(outer, inner, far, near, w_mix, w_context)
+
+
+def post_kernel(layer, last, lengths_ref, base_ref, parts, gains, w_up, w_down, *refs):
+    *refs, base, base_sems, lengths, lengths_sem = refs
     users = base.shape[0]
+    get_lengths = pltpu.make_async_copy(lengths_ref, lengths, lengths_sem)
 
     def fetch(i):
         part = pl.ds(i * PIECE, PIECE)
         return pltpu.make_async_copy(base_ref.at[part], base.at[part], base_sems.at[i])
 
-    for i in range(users // PIECE):
+    for i in range(STEP // PIECE):
+        fetch(i).start()
+    get_lengths.start()
+    for i in range(STEP // PIECE, users // PIECE):
         fetch(i).start()
     if last:
         out_ref, out_buf, add, sems = refs
     else:
-        w_ref, head_ref, tail_ref, totals_ref, add, sums, w, sem = refs
+        w_ref, outer_ref, inner_ref, totals_ref, add, sums, w, sem = refs
         get_w = pltpu.make_async_copy(w_ref.at[layer + 1], w, sem)
         get_w.start()
     first_pos = first_position()
     t, scale = scale_rows(first_pos)
     add[...] = jnp.sum(parts[...].astype(F32), axis=0)
     gain = gains[layer : layer + 1]
+    starts = half_starts()
+    get_lengths.wait()
 
     def store(i):
         part = pl.ds(i * PIECE, PIECE)
@@ -260,12 +280,13 @@
                 t < lengths[u] - first_pos, result[k * ROWS : (k + 1) * ROWS], 0.0
             ).astype(BF16)
             if last:
-                out_buf[u] = state
+                out_buf[u, pl.ds(starts[0], HALF)] = state[:HALF]
+                out_buf[u, pl.ds(starts[1], HALF)] = state[HALF:]
                 if k % PIECE == PIECE - 1:
                     store(i * (STEP // PIECE) + k // PIECE).start()
             else:
-                head_ref[u] = state[:HALF]
-                tail_ref[u] = state[HALF:]
+                outer_ref[u] = state[:HALF]
+                inner_ref[u] = state[HALF:]
                 rows.append(jnp.sum(state.astype(F32), axis=0, keepdims=True))
         if not last:
             sums[pl.ds(b, STEP)] = jnp.concatenate(rows, axis=0)
@@ -284,8 +305,8 @@
 
 def post(layer, last, copies, lengths, base, parts, w_context, gains, w_up, w_down):
     users = base.shape[0]
-    in_specs = [SMEM, HBM] + [VMEM] * 4
-    args = (lengths, in_hbm(base), parts, gains, w_up, w_down)
+    in_specs = [HBM, HBM] + [VMEM] * 4
+    args = (in_hbm(lengths), in_hbm(base), parts, gains, w_up, w_down)
     if last:
         out_specs = HBM
         out_shape = jax.ShapeDtypeStruct((users, ROWS, D), BF16)
@@ -306,7 +327,12 @@
             pltpu.VMEM((D, D), BF16),
             pltpu.SemaphoreType.DMA,
         ]
-    scratch += [pltpu.VMEM((users, ROWS, D), F32), pltpu.SemaphoreType.DMA((users // PIECE,))]
+    scratch += [
+        pltpu.VMEM((users, ROWS, D), F32),
+        pltpu.SemaphoreType.DMA((users // PIECE,)),
+        pltpu.SMEM(lengths.shape, jnp.int32),
+        pltpu.SemaphoreType.DMA,
+    ]
     return pl.pallas_call(
         functools.partial(post_kernel, layer, last),
         in_specs=in_specs,
@@ -338,26 +364,29 @@
     return sent.astype(BF16)
 
 
-def halos(head, tail):
+def halos(outer, inner):
     n = lax.axis_size(TM)
-    up = [(i, i + 1) for i in range(n - 1)]
-    down = [(i + 1, i) for i in range(n - 1)]
-    return lax.ppermute(tail, TM, up), lax.ppermute(head, TM, down)
+
+    def swapped(first):
+        pairs = [(i, i + 1) for i in range(first, n - 1, 2)]
+        return pairs + [(j, i) for i, j in pairs]
+
+    return lax.ppermute(outer, TM, swapped(1)), lax.ppermute(inner, TM, swapped(0))
 
 
 def per_device(events, lengths, w_mix, w_context, gains, w_up, w_down):
     copies = lax.axis_size(("tm_0", "tm_2"))
     w_mix, w_context = in_hbm(w_mix), in_hbm(w_context)
-    head, tail, totals = pre(in_hbm(events), in_hbm(lengths), w_context, copies)
+    outer, inner, totals = pre(in_hbm(events), in_hbm(lengths), w_context, copies)
     for layer in range(LAYERS):
         last = layer == LAYERS - 1
-        low, high = halos(head, tail)
+        far, near = halos(outer, inner)
         parts = lax.all_to_all(messages(totals), "tm_1", 0, 0, tiled=True)
-        base = mix(layer, head, tail, low, high, w_mix, w_context)
+        base = mix(layer, outer, inner, far, near, w_mix, w_context)
         out = post(layer, last, copies, lengths, base, parts, w_context, gains, w_up, w_down)
         if last:
             return out
-        head, tail, totals = out
+        outer, inner, totals = out
 
 
 def solution(mesh):

time: 74.3 us -> 71.2 us (0.958)
  waiting for transfers between devices: 13.3 us -> 11.2 us
  Pallas kernels: 22.7 us -> 21.5 us
    ppermute x4, waiting for transfers between devices: 13.3 us -> 4.58 us  [the longest x2 4.57 us: halos(): lax.ppermute(outer, TM, swapped(1))]
    all_to_all x2, waiting for transfers between devices: 0.01 us -> 6.59 us  [per_device(): parts = lax.all_to_all(messages(totals), 'tm_1', 0, 0, tiled=True)]
    pallas_call x2, Pallas kernels: 12 us -> 10.9 us  [post(): pl.pallas_call(functools.partial(post_kernel, layer, last), in_specs=in_s...]
  transfers between devices with their start and end apart: 8 -> 8, of which waited for: 2 -> 4; matrix products, arithmetic and copies ran while one was open for 3% -> 3% of each run, Pallas kernels for 12% -> 12%
where the time goes in v2:
time: 71.2 us; the launch traced here: 70.4 us
  starting transfers between devices  35.3 us (50%)
  Pallas kernels  21.5 us (30%)
  waiting for transfers between devices  11.2 us (16%)
  other arithmetic  1.79 us (3%)
    ppermute x2, starting transfers between devices, halos(): lax.ppermute(outer, TM, swapped(1))  12.6 us
    all_to_all x2, starting transfers between devices, messages(): got = lax.all_to_all(totals, ('tm_0', 'tm_2'), 0, 0, tiled=True)  11.3 us
    pallas_call x2, Pallas kernels, post(): pl.pallas_call(functools.partial(post_kernel, layer, last), in_specs=in_s...  10.9 us
    pallas_call x2, Pallas kernels, mix(): pl.pallas_call(functools.partial(mix_kernel, layer), in_specs=[VMEM] * 2...  8.43 us
    all_to_all x2, starting transfers between devices, per_device(): parts = lax.all_to_all(messages(totals), 'tm_1', 0, 0, tiled=True)  6.84 us
    all_to_all x2, waiting for transfers between devices, per_device(): parts = lax.all_to_all(messages(totals), 'tm_1', 0, 0, tiled=True)  6.59 us
    ppermute x2, waiting for transfers between devices, halos(): lax.ppermute(outer, TM, swapped(1))  4.57 us
    ppermute x2, starting transfers between devices, halos(): lax.ppermute(inner, TM, swapped(0))  4.51 us
  transfers between devices with their start and end apart: 8, of which 4 were waited for; matrix products, arithmetic and copies ran while one was open for 3% of the time, Pallas kernels for 12%

profile of v2, /device:TPU:56, one launch (start us, length us, event | category | flops | bytes accessed | tf_op | source)
XLA Modules:
  0.0 70.4 jit_solution(14867212716991270248)
XLA Ops:
  0.0 2.2 %pre.1 = (bf16[32,32,256]{2,1,0:T(8,128)(2,1)S(1)}, bf16[32,32,256]{2,1,0:T(8,128)(2,1)S(1)}, bf16[8,32,256]{2,1,0:T(8,128)(2,1)}) custom-call(bf16[32,64,256]{2,1,0:T(8,128)(2,1)} %events_ref.1, s32[32]{0:T(128)} %lengths_ref.5, bf16[2,256,256]{2,1,0:T(8,128)(2,1)} %w_context.3), custom_call_target="tpu_custom_call" | custom-call | flops 1048576 | bytes 2097152 | tf_op jit(solution)/shard_map/pre/pallas_call | solution.py:103
  2.2 6.2 %all-to-all-start = ((bf16[8,32,256]{2,1,0:T(8,128)(2,1)}), bf16[8,32,256]{2,1,0:T(8,128)(2,1)S(1)}, u32[]{:S(2)}, u32[]{:S(2)}) async-start(bf16[8,32,256]{2,1,0:T(8,128)(2,1)} %get-tuple-element.13), calls=%async_computation | async-start | bytes 262144 | tf_op jit(solution)/shard_map/all_to_all | solution.py:355
  8.4 10.7 %collective-permute-start = (bf16[32,32,256]{2,1,0:T(8,128)(2,1)S(1)}, bf16[32,32,256]{2,1,0:T(8,128)(2,1)}, u32[]{:S(2)}, u32[]{:S(2)}) collective-permute-start(bf16[32,32,256]{2,1,0:T(8,128)(2,1)S(1)} %get-tuple-element.11.outer), channel_id=1, source_target_pairs={{8,16},{24,32},{40,48},{56,64},{72,80},{88,96},{104,112},{120,128}... | collective-permute-start | bytes 1572872 | tf_op jit(solution)/shard_map/ppermute | solution.py:374
  19.1 1.9 %collective-permute-start.1 = (bf16[32,32,256]{2,1,0:T(8,128)(2,1)S(1)}, bf16[32,32,256]{2,1,0:T(8,128)(2,1)}, u32[]{:S(2)}, u32[]{:S(2)}) collective-permute-start(bf16[32,32,256]{2,1,0:T(8,128)(2,1)S(1)} %get-tuple-element.12.inner), channel_id=1, source_target_pairs={{0,8},{16,24},{32,40},{48,56},{64,72},{80,88},{96,104},{112,120},{... | collective-permute-start | bytes 1572872 | tf_op jit(solution)/shard_map/ppermute | solution.py:374
  21.1 0.1 and.29
  21.2 0.1 broadcast_in_dim.117
  21.4 0.1 broadcast_in_dim.112
  21.5 0.1 fusion
  21.6 0.8 %add_convert_fusion.1 = bf16[8,32,256]{2,1,0:T(8,128)(2,1)} fusion(f32[32,256]{1,0:T(8,128)S(1)} %get-tuple-element.22, f32[32,256]{1,0:T(8,128)S(1)} %get-tuple-element.21, f32[32,256]{1,0:T(8,128)S(1)} %get-tuple-element.20, pred[8]{0:T(512)(128)(4,1)S(1)} %get-tuple-element.25, pred[8]{0:T(512)(128)(4,1)S(1)} %get-tuple-element.26), kind=kLoop, calls=%fused_computation.13 | loop fusion | flops 262144 | bytes 229392 | tf_op jit(solution)/shard_map/convert_element_type | solution.py:364
  22.4 3.4 %all-to-all-start.1 = ((bf16[8,32,256]{2,1,0:T(8,128)(2,1)}), bf16[8,32,256]{2,1,0:T(8,128)(2,1)S(1)}, u32[]{:S(2)}, u32[]{:S(2)}) async-start(bf16[8,32,256]{2,1,0:T(8,128)(2,1)} %add_convert_fusion.1), calls=%async_computation.1 | async-start | bytes 262144 | tf_op jit(solution)/shard_map/all_to_all | solution.py:384
  25.8 0.8 %collective-permute-done.far_ref = bf16[32,32,256]{2,1,0:T(8,128)(2,1)} collective-permute-done((bf16[32,32,256]{2,1,0:T(8,128)(2,1)S(1)}, bf16[32,32,256]{2,1,0:T(8,128)(2,1)}, u32[]{:S(2)}, u32[]{:S(2)}) %collective-permute-start) | collective-permute-done | bytes 524320 | tf_op jit(solution)/shard_map/ppermute | solution.py:374
  26.6 4.2 %mix.2.base_ref = f32[32,64,256]{2,1,0:T(8,128)} custom-call(bf16[32,32,256]{2,1,0:T(8,128)(2,1)S(1)} %get-tuple-element.11.outer, bf16[32,32,256]{2,1,0:T(8,128)(2,1)S(1)} %get-tuple-element.12.inner, bf16[32,32,256]{2,1,0:T(8,128)(2,1)} %collective-permute-done.far_ref, bf16[32,32,256]{2,1,0:T(8,128)(2,1)} %collective-permute-done.1.near_ref, ...), custom_call_target="tpu_custom_call" | custom-call | flops 1342177280 | bytes 4194304 | tf_op jit(solution)/shard_map/mix/pallas_call | solution.py:205
  30.8 4.9 %all-to-all-done.1.parts = bf16[8,32,256]{2,1,0:T(8,128)(2,1)S(1)} async-done(((bf16[8,32,256]{2,1,0:T(8,128)(2,1)}), bf16[8,32,256]{2,1,0:T(8,128)(2,1)S(1)}, u32[]{:S(2)}, u32[]{:S(2)}) %all-to-all-start.1) | async-done | bytes 131104 | tf_op jit(solution)/shard_map/all_to_all | solution.py:384
  35.7 5.5 %post.2 = (bf16[32,32,256]{2,1,0:T(8,128)(2,1)S(1)}, bf16[32,32,256]{2,1,0:T(8,128)(2,1)S(1)}, bf16[8,32,256]{2,1,0:T(8,128)(2,1)}) custom-call(s32[32]{0:T(128)} %lengths_ref.5, f32[32,64,256]{2,1,0:T(8,128)} %mix.2.base_ref, bf16[8,32,256]{2,1,0:T(8,128)(2,1)S(1)} %all-to-all-done.1.parts, f32[2,256]{1,0:T(2,128)S(1)} %copy-done.2, ...), custom_call_target="tpu_custom_call" | custom-call | flops 2147483648 | bytes 3145728 | tf_op jit(solution)/shard_map/post/pallas_call | solution.py:336
  41.3 5.1 %all-to-all-start.2 = ((bf16[8,32,256]{2,1,0:T(8,128)(2,1)}), bf16[8,32,256]{2,1,0:T(8,128)(2,1)S(1)}, u32[]{:S(2)}, u32[]{:S(2)}) async-start(bf16[8,32,256]{2,1,0:T(8,128)(2,1)} %get-tuple-element.16), calls=%async_computation.2 | async-start | bytes 262144 | tf_op jit(solution)/shard_map/all_to_all | solution.py:355
  46.4 1.9 %collective-permute-start.2 = (bf16[32,32,256]{2,1,0:T(8,128)(2,1)S(1)}, bf16[32,32,256]{2,1,0:T(8,128)(2,1)}, u32[]{:S(2)}, u32[]{:S(2)}) collective-permute-start(bf16[32,32,256]{2,1,0:T(8,128)(2,1)S(1)} %get-tuple-element.14.outer), channel_id=1, source_target_pairs={{8,16},{24,32},{40,48},{56,64},{72,80},{88,96},{104,112},{120,128}... | collective-permute-start | bytes 1572872 | tf_op jit(solution)/shard_map/ppermute | solution.py:374
  48.3 2.6 %collective-permute-start.3 = (bf16[32,32,256]{2,1,0:T(8,128)(2,1)S(1)}, bf16[32,32,256]{2,1,0:T(8,128)(2,1)}, u32[]{:S(2)}, u32[]{:S(2)}) collective-permute-start(bf16[32,32,256]{2,1,0:T(8,128)(2,1)S(1)} %get-tuple-element.15.inner), channel_id=1, source_target_pairs={{0,8},{16,24},{32,40},{48,56},{64,72},{80,88},{96,104},{112,120},{... | collective-permute-start | bytes 1572872 | tf_op jit(solution)/shard_map/ppermute | solution.py:374
  50.9 0.1 fusion.3
  51.0 0.8 %add_convert_fusion = bf16[8,32,256]{2,1,0:T(8,128)(2,1)} fusion(f32[32,256]{1,0:T(8,128)S(1)} %get-tuple-element.19, f32[32,256]{1,0:T(8,128)S(1)} %get-tuple-element.18, f32[32,256]{1,0:T(8,128)S(1)} %get-tuple-element.17, pred[8]{0:T(512)(128)(4,1)S(1)} %get-tuple-element.25, pred[8]{0:T(512)(128)(4,1)S(1)} %get-tuple-element.26), kind=kLoop, calls=%fused_computation.12 | loop fusion | flops 262144 | bytes 229392 | tf_op jit(solution)/shard_map/convert_element_type | solution.py:364
  51.8 3.5 %all-to-all-start.3 = ((bf16[8,32,256]{2,1,0:T(8,128)(2,1)}), bf16[8,32,256]{2,1,0:T(8,128)(2,1)S(1)}, u32[]{:S(2)}, u32[]{:S(2)}) async-start(bf16[8,32,256]{2,1,0:T(8,128)(2,1)} %add_convert_fusion), calls=%async_computation.3 | async-start | bytes 262144 | tf_op jit(solution)/shard_map/all_to_all | solution.py:384
  55.3 3.8 %collective-permute-done.2.far_ref = bf16[32,32,256]{2,1,0:T(8,128)(2,1)} collective-permute-done((bf16[32,32,256]{2,1,0:T(8,128)(2,1)S(1)}, bf16[32,32,256]{2,1,0:T(8,128)(2,1)}, u32[]{:S(2)}, u32[]{:S(2)}) %collective-permute-start.2) | collective-permute-done | bytes 524320 | tf_op jit(solution)/shard_map/ppermute | solution.py:374
  59.1 4.2 %mix.3.base_ref = f32[32,64,256]{2,1,0:T(8,128)} custom-call(bf16[32,32,256]{2,1,0:T(8,128)(2,1)S(1)} %get-tuple-element.14.outer, bf16[32,32,256]{2,1,0:T(8,128)(2,1)S(1)} %get-tuple-element.15.inner, bf16[32,32,256]{2,1,0:T(8,128)(2,1)} %collective-permute-done.2.far_ref, bf16[32,32,256]{2,1,0:T(8,128)(2,1)} %collective-permute-done.3.near_ref, ...), custom_call_target="tpu_custom_call" | custom-call | flops 1342177280 | bytes 4194304 | tf_op jit(solution)/shard_map/mix/pallas_call | solution.py:205
  63.3 1.7 %all-to-all-done.3.parts = bf16[8,32,256]{2,1,0:T(8,128)(2,1)S(1)} async-done(((bf16[8,32,256]{2,1,0:T(8,128)(2,1)}), bf16[8,32,256]{2,1,0:T(8,128)(2,1)S(1)}, u32[]{:S(2)}, u32[]{:S(2)}) %all-to-all-start.3) | async-done | bytes 131104 | tf_op jit(solution)/shard_map/all_to_all | solution.py:384
  65.0 5.4 %post.3 = bf16[32,64,256]{2,1,0:T(8,128)(2,1)} custom-call(s32[32]{0:T(128)} %lengths_ref.5, f32[32,64,256]{2,1,0:T(8,128)} %mix.3.base_ref, bf16[8,32,256]{2,1,0:T(8,128)(2,1)S(1)} %all-to-all-done.3.parts, f32[2,256]{1,0:T(2,128)S(1)} %copy-done.2, bf16[2,256,1024]{2,1,0:T(8,128)(2,1)S(1)} %copy-done, bf16[2,1024,256]{2,1,0:T(8,128)(2,1)S(1)} %copy-done.1), custom_call_target="tpu_custom_call" | custom-call | flops 2147483648 | bytes 3145728 | tf_op jit(solution)/shard_map/post/pallas_call | solution.py:336
  (17 shorter events, 0.2 us)
Async XLA Ops:
  2.2 19.3 %all-to-all-start = ((bf16[8,32,256]{2,1,0:T(8,128)(2,1)}), bf16[8,32,256]{2,1,0:T(8,128)(2,1)S(1)}, u32[]{:S(2)}, u32[]{:S(2)}) async-start(bf16[8,32,256]{2,1,0:T(8,128)(2,1)} %get-tuple-element.13), calls=%async_computation | async-start | bytes 262144 | tf_op jit(solution)/shard_map/all_to_all | solution.py:355
  8.4 18.2 %collective-permute-start = (bf16[32,32,256]{2,1,0:T(8,128)(2,1)S(1)}, bf16[32,32,256]{2,1,0:T(8,128)(2,1)}, u32[]{:S(2)}, u32[]{:S(2)}) collective-permute-start(bf16[32,32,256]{2,1,0:T(8,128)(2,1)S(1)} %get-tuple-element.11.outer), channel_id=1, source_target_pairs={{8,16},{24,32},{40,48},{56,64},{72,80},{88,96},{104,112},{120,128}... | collective-permute-start | bytes 1572872 | tf_op jit(solution)/shard_map/ppermute | solution.py:374
  19.1 7.5 %collective-permute-start.1 = (bf16[32,32,256]{2,1,0:T(8,128)(2,1)S(1)}, bf16[32,32,256]{2,1,0:T(8,128)(2,1)}, u32[]{:S(2)}, u32[]{:S(2)}) collective-permute-start(bf16[32,32,256]{2,1,0:T(8,128)(2,1)S(1)} %get-tuple-element.12.inner), channel_id=1, source_target_pairs={{0,8},{16,24},{32,40},{48,56},{64,72},{80,88},{96,104},{112,120},{... | collective-permute-start | bytes 1572872 | tf_op jit(solution)/shard_map/ppermute | solution.py:374
  22.4 13.3 %all-to-all-start.1 = ((bf16[8,32,256]{2,1,0:T(8,128)(2,1)}), bf16[8,32,256]{2,1,0:T(8,128)(2,1)S(1)}, u32[]{:S(2)}, u32[]{:S(2)}) async-start(bf16[8,32,256]{2,1,0:T(8,128)(2,1)} %add_convert_fusion.1), calls=%async_computation.1 | async-start | bytes 262144 | tf_op jit(solution)/shard_map/all_to_all | solution.py:384
  25.8 9.9 %copy-start = (bf16[2,256,1024]{2,1,0:T(8,128)(2,1)S(1)}, bf16[2,256,1024]{2,1,0:T(8,128)(2,1)}, u32[]{:S(2)}) copy-start(bf16[2,256,1024]{2,1,0:T(8,128)(2,1)} %w_up.3) | copy-start | bytes 3145732
  25.8 9.9 %copy-start.1 = (bf16[2,1024,256]{2,1,0:T(8,128)(2,1)S(1)}, bf16[2,1024,256]{2,1,0:T(8,128)(2,1)}, u32[]{:S(2)}) copy-start(bf16[2,1024,256]{2,1,0:T(8,128)(2,1)} %w_down.3) | copy-start | bytes 3145732
  25.8 9.9 %copy-start.2 = (f32[2,256]{1,0:T(2,128)S(1)}, f32[2,256]{1,0:T(2,128)}, u32[]{:S(2)}) copy-start(f32[2,256]{1,0:T(2,128)} %gains.3) | copy-start | bytes 6148
  41.3 9.6 %all-to-all-start.2 = ((bf16[8,32,256]{2,1,0:T(8,128)(2,1)}), bf16[8,32,256]{2,1,0:T(8,128)(2,1)S(1)}, u32[]{:S(2)}, u32[]{:S(2)}) async-start(bf16[8,32,256]{2,1,0:T(8,128)(2,1)} %get-tuple-element.16), calls=%async_computation.2 | async-start | bytes 262144 | tf_op jit(solution)/shard_map/all_to_all | solution.py:355
  46.4 12.7 %collective-permute-start.2 = (bf16[32,32,256]{2,1,0:T(8,128)(2,1)S(1)}, bf16[32,32,256]{2,1,0:T(8,128)(2,1)}, u32[]{:S(2)}, u32[]{:S(2)}) collective-permute-start(bf16[32,32,256]{2,1,0:T(8,128)(2,1)S(1)} %get-tuple-element.14.outer), channel_id=1, source_target_pairs={{8,16},{24,32},{40,48},{56,64},{72,80},{88,96},{104,112},{120,128}... | collective-permute-start | bytes 1572872 | tf_op jit(solution)/shard_map/ppermute | solution.py:374
  48.3 10.8 %collective-permute-start.3 = (bf16[32,32,256]{2,1,0:T(8,128)(2,1)S(1)}, bf16[32,32,256]{2,1,0:T(8,128)(2,1)}, u32[]{:S(2)}, u32[]{:S(2)}) collective-permute-start(bf16[32,32,256]{2,1,0:T(8,128)(2,1)S(1)} %get-tuple-element.15.inner), channel_id=1, source_target_pairs={{0,8},{16,24},{32,40},{48,56},{64,72},{80,88},{96,104},{112,120},{... | collective-permute-start | bytes 1572872 | tf_op jit(solution)/shard_map/ppermute | solution.py:374
  51.8 13.2 %all-to-all-start.3 = ((bf16[8,32,256]{2,1,0:T(8,128)(2,1)}), bf16[8,32,256]{2,1,0:T(8,128)(2,1)S(1)}, u32[]{:S(2)}, u32[]{:S(2)}) async-start(bf16[8,32,256]{2,1,0:T(8,128)(2,1)} %add_convert_fusion), calls=%async_computation.3 | async-start | bytes 262144 | tf_op jit(solution)/shard_map/all_to_all | solution.py:384
